TPU v7x, 32 devices: a whole 2x2x4 slice. The times are simulated.
32 devices in a mesh: grp: 2 (over x), fsdp: 4 (over z), tp: 4 (over y, core).
Axes of the slice: x: 2, y: 2, z: 4, core: 2. Of those that a mesh axis runs over, the one named last changes fastest.
Arguments:
- learn_hidden: bfloat16 [8192, 14336], P(('grp', 'fsdp'), 'tp'), may hold values from -6 to 6
- learn_cotangent: bfloat16 [8192, 4096], P(('grp', 'fsdp')), may hold values from -0.09375 to 0.09375
- master_weight: float32 [4096, 14336], P(('grp', 'fsdp'), 'tp'), may hold values from -0.046875 to 0.046875
- momentum: float32 [4096, 14336], P(('grp', 'fsdp'), 'tp'), may hold values from -6 to 6
- roll_hidden: bfloat16 [256, 14336], P(('grp', 'fsdp'), 'tp'), may hold values from -6 to 6
Outputs:
- momentum_new: float32 [4096, 14336], P(('grp', 'fsdp'), 'tp')
- roll_out: bfloat16 [256, 4096], P(('grp', 'fsdp'))
All inputs are finite; a program needn't handle non-finite values.
Results may differ from a plain program's by a relative error of at most 0.015.
Values may be sent and summed in bfloat16 or wider, within the bound.
A program may use at most 128 MiB of HBM per device.

v0:
```python
import jax
import jax.numpy as jnp
from jax import lax
from jax.sharding import PartitionSpec as P

MOMENTUM = 0.9
LEARN_RATE = 0.002


def local(learn_hidden, learn_cotangent, master_weight, momentum, roll_hidden):
    grad = lax.psum_scatter(
        lax.dot_general(
            learn_cotangent,
            learn_hidden,
            (((0,), (0,)), ((), ())),
            preferred_element_type=jnp.float32,
        ).astype(jnp.bfloat16),
        ("grp", "fsdp"),
        scatter_dimension=0,
        tiled=True,
    ).astype(jnp.float32)
    momentum_new = MOMENTUM * momentum + grad
    rollout_weight = (master_weight - LEARN_RATE * momentum_new).astype(jnp.bfloat16)
    partial_out = lax.dot_general(
        lax.all_gather(roll_hidden, ("grp", "fsdp"), axis=0, tiled=True),
        rollout_weight,
        (((1,), (1,)), ((), ())),
        preferred_element_type=jnp.float32,
    )
    column_sum = lax.psum(partial_out.astype(jnp.bfloat16), "tp").astype(jnp.float32)
    roll_sum = lax.all_to_all(
        column_sum.astype(jnp.bfloat16), ("grp", "fsdp"), split_axis=0, concat_axis=1, tiled=True
    ).astype(column_sum.dtype)
    roll_out = roll_sum.astype(jnp.bfloat16)
    return (momentum_new, roll_out)


def solution(mesh):
    placed = (
        P(("grp", "fsdp"), "tp"),
        P(("grp", "fsdp"), None),
        P(("grp", "fsdp"), "tp"),
        P(("grp", "fsdp"), "tp"),
        P(("grp", "fsdp"), "tp"),
    )
    return jax.shard_map(
        local,
        mesh=mesh,
        in_specs=placed,
        out_specs=(P(("grp", "fsdp"), "tp"), P(("grp", "fsdp"), None)),
        check_vma=False,
    )
```

profile of v0, /device:TPU:0, one launch (start us, length us, event | category | flops | bytes accessed | tf_op | source)
XLA Modules:
  0.0 619.6 jit_solution(11331522453792676685)
XLA Ops:
  7.2 0.0 reduce-scatter.2.cloned.1.call-start
  7.2 38.1 %convolution_convert_fusion = bf16[4096,3584]{1,0:T(8,128)(2,1)} fusion(bf16[1024,4096]{1,0:T(8,128)(2,1)} %param.6, bf16[1024,3584]{1,0:T(8,128)(2,1)} %param.5), kind=kOutput, calls=%fused_computation | convolution fusion | flops 30079451136 | bytes 45088768 | tf_op jit(solution)/shard_map/dot_general | solution.py:12
  45.4 0.0 reduce-scatter.2.cloned.1.call-update
  45.4 0.0 all-gather.2.cloned.1.call-start
  45.4 0.7 all-gather.2.cloned.1.call-update
  46.1 0.0 all-reduce.2.cloned.1.call-start
  46.2 465.5 %reduce-scatter.2.cloned.1.call-done = bf16[512,3584]{1,0:T(8,128)(2,1)} async-done(((bf16[4096,3584]{1,0:T(8,128)(2,1)}), bf16[512,3584]{1,0:T(8,128)(2,1)}) %reduce-scatter.2.cloned.1.call-update) | async-done | bytes 3670032 | tf_op jit(solution)/shard_map/reduce_scatter | solution.py:11
  511.7 8.3 %convert_add_fusion = f32[512,3584]{1,0:T(8,128)} fusion(bf16[512,3584]{1,0:T(8,128)(2,1)} %reduce-scatter.2.cloned.1.call-done, f32[512,3584]{1,0:T(8,128)} %param.8), kind=kLoop, calls=%fused_computation.2 | loop fusion | flops 5505024 | bytes 18350080 | tf_op jit(solution)/shard_map/add | solution.py:22
  520.0 39.3 %all-gather.2.cloned.1.call-done = bf16[256,3584]{1,0:T(8,128)(2,1)} async-done(((bf16[32,3584]{1,0:T(8,128)(2,1)}), bf16[256,3584]{1,0:T(8,128)(2,1)}) %all-gather.2.cloned.1.call-update) | async-done | bytes 1835024 | tf_op jit(solution)/shard_map/all_gather | solution.py:25
  559.3 7.6 %fusion.2 = bf16[512,256]{0,1:T(8,128)(2,1)} fusion(bf16[256,3584]{1,0:T(8,128)(2,1)} %all-gather.2.cloned.1.call-done, f32[512,3584]{1,0:T(8,128)} %param.7, f32[512,3584]{1,0:T(8,128)} %convert_add_fusion), kind=kOutput, calls=%fused_computation.5 | convolution fusion | flops 945160192 | bytes 16777216 | tf_op jit(solution)/shard_map/dot_general | solution.py:24
  566.9 0.0 all-reduce.2.cloned.1.call-update
  566.9 31.2 %all-reduce.2.cloned.1.call-done = bf16[8,32,512]{2,1,0:T(8,128)(2,1)} async-done(((bf16[8,32,512]{2,1,0:T(8,128)(2,1)}), bf16[8,32,512]{2,1,0:T(8,128)(2,1)}) %all-reduce.2.cloned.1.call-update) | async-done | bytes 262160 | tf_op jit(solution)/shard_map/psum | solution.py:30
  598.1 14.3 %all_to_all.19 = bf16[8,32,512]{2,1,0:T(8,128)(2,1)S(1)} all-to-all(bf16[8,32,512]{2,1,0:T(8,128)(2,1)} %all-reduce.2.cloned.1.call-done), channel_id=1, replica_groups=mesh['grp'=2,'fsdp'=4,'tp'=4] {'grp','fsdp'}, dimensions={0} | all-to-all | bytes 524288 | tf_op jit(solution)/shard_map/all_to_all | solution.py:31
  612.4 0.7 copy.8
Async XLA Ops:
  7.2 504.5 %reduce-scatter.2.cloned.1.call-start = ((), (), s32[]{:S(2)}) async-start(), calls=%async_computation.2 | async-start | bytes 33030144 | tf_op jit(solution)/shard_map/reduce_scatter | solution.py:11
  45.4 513.9 %all-gather.2.cloned.1.call-start = ((), (), s32[]{:S(2)}) async-start(), calls=%async_computation.3 | async-start | bytes 2064384 | tf_op jit(solution)/shard_map/all_gather | solution.py:25
  46.1 551.9 %all-reduce.2.cloned.1.call-start = ((), (), s32[]{:S(2)}) async-start(), calls=%async_computation.4 | async-start | bytes 524288 | tf_op jit(solution)/shard_map/psum | solution.py:30
Sparse Core Ops, SparseCore 0:
  45.5 466.1 reduce-scatter.1
  513.8 45.4 all-gather.1
  567.0 30.9 all-reduce.1
where the time goes:
time: 620 us
  waiting for transfers between devices  537 us (87%)
  matrix products  45.7 us (7%)
  blocking collectives  14.3 us (2%)
  between operations  13.7 us (2%)
  other arithmetic  8.33 us (1%)
    reduce_scatter x1, waiting for transfers between devices, local(): lax.psum_scatter(lax.dot_general(learn_cotangent, learn_hidden, (((0,), (...  466 us
    all_gather x1, waiting for transfers between devices, local(): lax.all_gather(roll_hidden, ('grp', 'fsdp'), axis=0, tiled=True)  39.3 us
    dot_general x1, matrix products, local(): lax.dot_general(learn_cotangent, learn_hidden, (((0,), (0,)), ((), ())),...  38.1 us
    psum x1, waiting for transfers between devices, local(): lax.psum(partial_out.astype(jnp.bfloat16), 'tp').astype(jnp.float32)  31.2 us
    all_to_all x1, blocking collectives, local(): lax.all_to_all(column_sum.astype(jnp.bfloat16), ('grp', 'fsdp'), split_ax...  14.3 us
  transfers between devices with their start and end apart: 3, of which 3 were waited for; matrix products, arithmetic and copies ran while one was open for 1% of the time, Pallas kernels for 0%

commit v1 on v0

v1 whole, which is shorter than its diff:
```python
import functools

import jax
import jax.numpy as jnp
from jax import lax
from jax.experimental import pallas as pl
from jax.experimental.pallas import tpu as pltpu
from jax.sharding import PartitionSpec as P

MESH = pl.DeviceIdType.MESH
MOMENTUM = 0.9
LEARN_RATE = 0.002
TOKENS_FIRST = (((0,), (0,)), ((), ()))
LAG = 2


def remote(src, dst, send_sem, recv_sem, target):
    return pltpu.make_async_remote_copy(
        src_ref=src, dst_ref=dst, send_sem=send_sem, recv_sem=recv_sem, device_id=target, device_id_type=MESH
    )


def grad_kernel(
    n, n_tp, cot_hbm, hid_hbm, grad_hbm,
    cot, own, other, term, recv, total,
    cot_local, own_sem, cot_send, cot_recv, hid_send, hid_recv, send_sem, recv_sem, out_sem,
):
    g, f, t = lax.axis_index("grp"), lax.axis_index("fsdp"), lax.axis_index("tp")
    chunks, tokens, width = own.shape
    rows = total.shape[0]
    half = n * rows
    share = tokens // n_tp
    pairs = n_tp // 2
    y, core = t // 2, t % 2
    peer = {"grp": 1 - g}
    partner = y * 2 + (1 - core)

    def mate(step):
        return lax.rem(y + step, pairs) * 2 + core

    barrier = pltpu.get_barrier_semaphore()
    pl.semaphore_signal(barrier, inc=1, device_id=peer, device_id_type=MESH)
    pl.semaphore_signal(barrier, inc=1, device_id={"tp": partner}, device_id_type=MESH)
    for step in range(1, pairs):
        pl.semaphore_signal(barrier, inc=1, device_id={"tp": mate(step)}, device_id_type=MESH)

    @pl.when(f > 0)
    def _():
        pl.semaphore_signal(barrier, inc=1, device_id={"fsdp": f - 1}, device_id_type=MESH)

    @pl.when(f < n - 1)
    def _():
        pl.semaphore_signal(barrier, inc=1, device_id={"fsdp": f + 1}, device_id_type=MESH)

    peers = 1 + pairs + (f > 0).astype(jnp.int32) + (f < n - 1).astype(jnp.int32)
    pl.semaphore_wait(barrier, peers)

    def cot_block(b):
        return cot.at[pl.ds(pl.multiple_of(tokens + b * share, share), share), :]

    def hid_cols(k):
        return hid_hbm.at[:, pl.ds(pl.multiple_of(k * width, width), width)]

    first_cot = remote(
        cot_hbm.at[pl.ds(pl.multiple_of(t * share, share), share), pl.ds(pl.multiple_of((1 - g) * half, half), half)],
        cot_block(t), cot_send.at[0], cot_recv.at[t], peer,
    )
    first_cot.start()

    def hidden_copy(k):
        return remote(hid_cols(k), other.at[k], hid_send.at[k], hid_recv.at[k], peer)

    def own_copy(k):
        return pltpu.make_async_copy(hid_cols(k), own.at[k], own_sem.at[k])

    def start_hidden(k, _):
        hidden_copy(k).start()
        return 0

    lax.fori_loop(0, chunks, start_hidden, 0)
    own_cot = pltpu.make_async_copy(
        cot_hbm.at[:, pl.ds(pl.multiple_of(g * half, half), half)], cot.at[pl.ds(0, tokens), :], cot_local.at[0]
    )
    own_cot.start()

    def start_own(k, _):
        own_copy(k).start()
        return 0

    lax.fori_loop(0, chunks, start_own, 0)

    first_cot.wait_recv()
    sends = []
    for step in range(1, pairs):
        sends.append(remote(cot_block(t), cot_block(t), cot_send.at[step], cot_recv.at[t], {"tp": mate(step)}))
        sends[-1].start()
    sends.append(remote(cot_block(t), cot_block(t), cot_send.at[pairs], cot_recv.at[t], {"tp": partner}))
    sends[-1].start()
    for step in range(1, pairs):
        b = mate(step)
        arrived = remote(cot_block(b), cot_block(b), cot_send.at[pairs + step], cot_recv.at[b], {"tp": partner})
        arrived.wait_recv()
        arrived.start()
        sends.append(arrived)
    for step in range(pairs):
        b = lax.rem(y + step, pairs) * 2 + (1 - core)
        remote(cot_block(b), cot_block(b), cot_send.at[0], cot_recv.at[b], {"tp": partner}).wait_recv()
    own_cot.wait()

    def up_copy(k, c):
        return remote(term.at[k, c], recv.at[k, c + 1], send_sem.at[k, c], recv_sem.at[k, c + 1], {"fsdp": lax.rem(f + 1, n)})

    def down_copy(k, c):
        return remote(term.at[k, c], recv.at[k, c], send_sem.at[k, c], recv_sem.at[k, c], {"fsdp": lax.rem(f + n - 1, n)})

    def arrived(k, slot):
        remote(term.at[k, 0], recv.at[k, slot], send_sem.at[k, 0], recv_sem.at[k, slot], {"fsdp": lax.rem(f + 1, n)}).wait_recv()

    def compute(k):
        own_copy(k).wait()
        hidden_copy(k).wait_recv()

        def one(i, _):
            c = jnp.where(f == n - 1, i, n - 1 - i)
            cols = pl.ds(pl.multiple_of(c * rows, rows), rows)
            value = lax.dot_general(
                cot[pl.ds(0, tokens), cols], own[k], TOKENS_FIRST, preferred_element_type=jnp.float32
            ) + lax.dot_general(
                cot[pl.ds(tokens, tokens), cols], other[k], TOKENS_FIRST, preferred_element_type=jnp.float32
            )
            term[k, c] = value.astype(jnp.bfloat16)

            @pl.when((f == 0) & (c > 0))
            def _():
                up_copy(k, c).start()

            @pl.when((f == n - 1) & (c < n - 1))
            def _():
                down_copy(k, c).start()

            return 0

        lax.fori_loop(0, n, one, 0)

    def relay(k):
        def one(i, _):
            c = n - 1 - i

            @pl.when((f > 0) & (c > f))
            def _():
                arrived(k, c + 1)
                term[k, c] = term[k, c] + recv[k, c + 1]
                up_copy(k, c).start()

            @pl.when((f < n - 1) & (i < f))
            def _():
                arrived(k, i)
                term[k, i] = term[k, i] + recv[k, i]
                down_copy(k, i).start()

            return 0

        lax.fori_loop(0, n, one, 0)

    def out_copy(k):
        return pltpu.make_async_copy(
            total, grad_hbm.at[:, pl.ds(pl.multiple_of(k * width, width), width)], out_sem.at[0]
        )

    def finish(k):
        @pl.when(f > 0)
        def _():
            arrived(k, f + 1)

        @pl.when(f < n - 1)
        def _():
            arrived(k, f)

        @pl.when(k > 0)
        def _():
            out_copy(k).wait()

        total[...] = term[k, f].astype(jnp.float32)

        @pl.when(f > 0)
        def _():
            total[...] += recv[k, f + 1].astype(jnp.float32)

        @pl.when(f < n - 1)
        def _():
            total[...] += recv[k, f].astype(jnp.float32)

        out_copy(k).start()

    def step(it, _):
        @pl.when(it < chunks)
        def _():
            compute(it)

        @pl.when((it >= 1) & (it <= chunks))
        def _():
            relay(it - 1)

        @pl.when(it >= LAG)
        def _():
            finish(it - LAG)

        return 0

    lax.fori_loop(0, chunks + LAG, step, 0)
    out_copy(0).wait()
    first_cot.wait_send()
    for copy in sends:
        copy.wait_send()

    def drain(k, _):
        hidden_copy(k).wait_send()

        def one(c, _):
            @pl.when(c != f)
            def _():
                up_copy(k, c).wait_send()

            return 0

        return lax.fori_loop(0, n, one, 0)

    lax.fori_loop(0, chunks, drain, 0)


def local(n_grp, n_fsdp, n_tp, learn_hidden, learn_cotangent, master_weight, momentum, roll_hidden):
    tokens, features = learn_cotangent.shape
    units = learn_hidden.shape[1]
    rows = features // n_grp // n_fsdp
    width = 256
    chunks = units // width
    pairs = n_tp // 2
    roll_all = lax.all_gather(roll_hidden, ("grp", "fsdp"), axis=0, tiled=True)
    dma = pltpu.SemaphoreType.DMA
    grad = pl.pallas_call(
        functools.partial(grad_kernel, n_fsdp, n_tp),
        out_shape=jax.ShapeDtypeStruct((rows, units), jnp.float32),
        in_specs=[pl.BlockSpec(memory_space=pl.ANY)] * 2,
        out_specs=pl.BlockSpec(memory_space=pl.ANY),
        scratch_shapes=[
            pltpu.VMEM((n_grp * tokens, features // n_grp), jnp.bfloat16),
            pltpu.VMEM((chunks, tokens, width), jnp.bfloat16),
            pltpu.VMEM((chunks, tokens, width), jnp.bfloat16),
            pltpu.VMEM((chunks, n_fsdp, rows, width), jnp.bfloat16),
            pltpu.VMEM((chunks, n_fsdp + 1, rows, width), jnp.bfloat16),
            pltpu.VMEM((rows, width), jnp.float32),
            dma((1,)),
            dma((chunks,)),
            dma((2 * pairs,)),
            dma((n_tp,)),
            dma((chunks,)),
            dma((chunks,)),
            dma((chunks, n_fsdp)),
            dma((chunks, n_fsdp + 1)),
            dma((1,)),
        ],
        compiler_params=pltpu.CompilerParams(
            collective_id=0, has_side_effects=True, vmem_limit_bytes=60 * 1024 * 1024
        ),
        name="grad_rows",
    )(learn_cotangent, learn_hidden)
    momentum_new = MOMENTUM * momentum + grad
    rollout_weight = (master_weight - LEARN_RATE * momentum_new).astype(jnp.bfloat16)
    partial_out = lax.dot_general(
        roll_all, rollout_weight, (((1,), (1,)), ((), ())), preferred_element_type=jnp.float32
    ).astype(jnp.bfloat16)
    spread = lax.all_to_all(partial_out, ("grp", "fsdp"), split_axis=0, concat_axis=1, tiled=True)
    roll_out = lax.psum(spread, "tp")
    return (momentum_new, roll_out)


def solution(mesh):
    blocks = P(("grp", "fsdp"), "tp")
    whole_rows = P(("grp", "fsdp"), None)
    sizes = (mesh.shape["grp"], mesh.shape["fsdp"], mesh.shape["tp"])
    return jax.shard_map(
        functools.partial(local, *sizes),
        mesh=mesh,
        in_specs=(blocks, whole_rows, blocks, blocks, blocks),
        out_specs=(blocks, whole_rows),
        check_vma=False,
    )
```

time: 620 us -> 388 us (0.63)
  waiting for transfers between devices: 537 us -> 30 us
  Pallas kernels: 0 us -> 314 us
  matrix products: 45.7 us -> 6.86 us
    reduce_scatter x1 -> x0, waiting for transfers between devices: 466 us -> none  [local(): lax.psum_scatter(lax.dot_general(learn_cotangent, learn_hidden, (((0,), (...]
    pallas_call x0 -> x1, Pallas kernels: none -> 314 us  [local(): pl.pallas_call(functools.partial(grad_kernel, n_fsdp, n_tp), out_shape=ja...]
    all_gather x1, waiting for transfers between devices: 39.3 us -> 0.01 us  [local(): roll_all = lax.all_gather(roll_hidden, ('grp', 'fsdp'), axis=0, tiled=True)]
    dot_general x2 -> x1, matrix products: 45.7 us -> 6.86 us  [local(): lax.dot_general(roll_all, rollout_weight, (((1,), (1,)), ((), ())), prefe...]
  transfers between devices with their start and end apart: 3 -> 2, of which waited for: 3 -> 1; matrix products, arithmetic and copies ran while one was open for 1% -> 2% of each run, Pallas kernels for 0% -> 81%
where the time goes in v1:
time: 388 us
  Pallas kernels  314 us (81%)
  waiting for transfers between devices  30 us (8%)
  between operations  14.1 us (4%)
  blocking collectives  11.2 us (3%)
  other arithmetic  9.68 us (2%)
  matrix products  6.86 us (2%)
    pallas_call x1, Pallas kernels, local(): pl.pallas_call(functools.partial(grad_kernel, n_fsdp, n_tp), out_shape=ja...  314 us
    psum x1, waiting for transfers between devices, local(): roll_out = lax.psum(spread, 'tp')  29.3 us
    all_to_all x1, blocking collectives, local(): lax.all_to_all(partial_out, ('grp', 'fsdp'), split_axis=0, concat_axis=1,...  11.2 us
    add x1, other arithmetic, local(): momentum_new = MOMENTUM * momentum + grad  9.68 us
  transfers between devices with their start and end apart: 2, of which 1 were waited for; matrix products, arithmetic and copies ran while one was open for 2% of the time, Pallas kernels for 81%

profile of v1, /device:TPU:0, one launch (start us, length us, event | category | flops | bytes accessed | tf_op | source)
XLA Modules:
  0.0 388.0 jit_solution(2384942209497356570)
XLA Ops:
  7.2 0.0 all-gather.2.cloned.1.call-start
  7.2 0.7 all-gather.2.cloned.1.call-update
  7.9 0.0 all-reduce.2.cloned.1.call-start
  7.9 313.7 %grad_rows.1 = f32[512,3584]{1,0:T(8,128)} custom-call(bf16[1024,4096]{1,0:T(8,128)(2,1)} %cot_hbm.1, bf16[1024,3584]{1,0:T(8,128)(2,1)} %hid_hbm.1), custom_call_target="tpu_custom_call" | custom-call | tf_op jit(solution)/shard_map/grad_rows/pallas_call | solution.py:240
  321.7 9.7 %multiply_add_fusion = f32[512,3584]{1,0:T(8,128)} fusion(f32[512,3584]{1,0:T(8,128)} %grad_rows.1, f32[512,3584]{1,0:T(8,128)} %param.8), kind=kLoop, calls=%fused_computation.1 | loop fusion | flops 3670016 | bytes 22020096 | tf_op jit(solution)/shard_map/add | solution.py:267
  331.4 0.0 all-gather.2.cloned.1.call-done
  331.4 6.9 %fusion.2 = bf16[512,256]{0,1:T(8,128)(2,1)S(1)} fusion(bf16[256,3584]{1,0:T(8,128)(2,1)} %all-gather.2.cloned.1.call-done, f32[512,3584]{1,0:T(8,128)} %param.7, f32[512,3584]{1,0:T(8,128)} %multiply_add_fusion), kind=kOutput, calls=%fused_computation.4 | convolution fusion | flops 945160192 | bytes 16777216 | tf_op jit(solution)/shard_map/dot_general | solution.py:269
  338.2 11.2 %all_to_all.19 = bf16[8,32,512]{2,1,0:T(8,128)(2,1)S(1)} all-to-all(bf16[8,32,512]{2,1,0:T(8,128)(2,1)S(1)} %bitcast.7), channel_id=1, replica_groups=mesh['grp'=2,'fsdp'=4,'tp'=4] {'grp','fsdp'}, dimensions={0} | all-to-all | bytes 524288 | tf_op jit(solution)/shard_map/all_to_all | solution.py:272
  349.5 0.7 copy.8
  350.2 0.0 all-reduce.2.cloned.1.call-update
  350.2 29.3 %all-reduce.2.cloned.1.call-done = bf16[32,4096]{1,0:T(8,128)(2,1)} async-done(((bf16[32,4096]{1,0:T(8,128)(2,1)}), bf16[32,4096]{1,0:T(8,128)(2,1)}) %all-reduce.2.cloned.1.call-update) | async-done | bytes 262160 | tf_op jit(solution)/shard_map/psum | solution.py:273
  379.5 1.7 copy.10
Async XLA Ops:
  7.2 324.2 %all-gather.2.cloned.1.call-start = ((), (), s32[]{:S(2)}) async-start(), calls=%async_computation.1 | async-start | bytes 2064384 | tf_op jit(solution)/shard_map/all_gather | solution.py:238
  7.9 371.6 %all-reduce.2.cloned.1.call-start = ((), (), s32[]{:S(2)}) async-start(), calls=%async_computation.2 | async-start | bytes 524288 | tf_op jit(solution)/shard_map/psum | solution.py:273
Sparse Core Ops, SparseCore 0:
  10.1 63.3 all-gather.1
  350.3 29.1 all-reduce.1

commit v2 on v1

v2 whole, which is shorter than its diff:
```python
import functools

import jax
import jax.numpy as jnp
from jax import lax
from jax.experimental import pallas as pl
from jax.experimental.pallas import tpu as pltpu
from jax.sharding import PartitionSpec as P

MESH = pl.DeviceIdType.MESH
MOMENTUM = 0.9
LEARN_RATE = 0.002
TOKENS_FIRST = (((0,), (0,)), ((), ()))
END_LAG = 4
MID_LAG = 3


def remote(src, dst, send_sem, recv_sem, target):
    return pltpu.make_async_remote_copy(
        src_ref=src, dst_ref=dst, send_sem=send_sem, recv_sem=recv_sem, device_id=target, device_id_type=MESH
    )


def step_kernel(
    n, n_tp, cot_hbm, hid_hbm, weight_hbm, momentum_hbm, roll_hbm, new_hbm, out_ref,
    cot, own, other, term, recv, total, held, master, rolls, acc, parts, landed, reduced, final,
    cot_local, own_sem, cot_send, cot_recv, hid_send, hid_recv, send_sem, recv_sem, out_sem, in_sem,
    roll_send, roll_recv, tail_send, all_recv, sum_recv, gather_recv,
):
    g, f, t = lax.axis_index("grp"), lax.axis_index("fsdp"), lax.axis_index("tp")
    chunks, tokens, width = own.shape
    rows = total.shape[0]
    half = n * rows
    share = tokens // n_tp
    pairs = n_tp // 2
    y, core = t // 2, t % 2
    peer = {"grp": 1 - g}
    partner = y * 2 + (1 - core)

    def mate(step):
        return lax.rem(y + step, pairs) * 2 + core

    groups = 2 * n
    me = g * n + f
    batch = roll_hbm.shape[0]

    def place(index):
        return {"grp": index // n, "fsdp": lax.rem(index, n)}

    barrier = pltpu.get_barrier_semaphore()
    for step in range(1, groups):
        pl.semaphore_signal(barrier, inc=1, device_id=place(lax.rem(me + step, groups)), device_id_type=MESH)
    for step in range(1, n_tp):
        pl.semaphore_signal(barrier, inc=1, device_id={"tp": lax.rem(t + step, n_tp)}, device_id_type=MESH)
    pl.semaphore_wait(barrier, groups + n_tp - 2)

    def order(i):
        return jnp.where(f >= n // 2, i, n - 1 - i)

    def cot_block(c, b):
        return cot.at[
            pl.ds(pl.multiple_of(tokens + b * share, share), share), pl.ds(pl.multiple_of(c * rows, rows), rows)
        ]

    def hid_cols(k):
        return hid_hbm.at[:, pl.ds(pl.multiple_of(k * width, width), width)]

    def cot_copy(c):
        return remote(
            cot_hbm.at[
                pl.ds(pl.multiple_of(t * share, share), share),
                pl.ds(pl.multiple_of((1 - g) * half + c * rows, rows), rows),
            ],
            cot_block(c, t), cot_send.at[c, 0], cot_recv.at[c, t], peer,
        )

    def hidden_copy(k):
        return remote(hid_cols(k), other.at[k], hid_send.at[k], hid_recv.at[k], peer)

    def own_copy(k):
        return pltpu.make_async_copy(hid_cols(k), own.at[k], own_sem.at[k])

    def start_hidden(k, _):
        hidden_copy(k).start()
        return 0

    cot_copy(order(0)).start()
    hidden_copy(0).start()
    for i in range(1, n):
        cot_copy(order(i)).start()
    early = min(chunks, 6)
    lax.fori_loop(1, early, start_hidden, 0)
    own_cot = pltpu.make_async_copy(
        cot_hbm.at[:, pl.ds(pl.multiple_of(g * half, half), half)], cot.at[pl.ds(0, tokens), :], cot_local.at[0]
    )
    own_cot.start()

    def start_own(k, _):
        own_copy(k).start()
        return 0

    lax.fori_loop(0, chunks, start_own, 0)

    def roll_block(index):
        return rolls.at[pl.ds(pl.multiple_of(index * batch, batch), batch), :]

    own_roll = pltpu.make_async_copy(roll_hbm, roll_block(me), in_sem.at[2])
    own_roll.start()

    def roll_copy(step):
        return remote(
            roll_hbm, roll_block(me), roll_send.at[step], roll_recv.at[me], {"fsdp": lax.rem(f + step, n)}
        )

    for step in range(1, n):
        roll_copy(step).start()

    def cross_copy(step):
        index = g * n + lax.rem(f + step, n)
        return remote(roll_block(index), roll_block(index), roll_send.at[n + step], roll_recv.at[index], peer)

    def roll_arrived(index):
        remote(roll_block(index), roll_block(index), roll_send.at[0], roll_recv.at[index], peer).wait_recv()

    def mate_copy(c, step):
        return remote(cot_block(c, t), cot_block(c, t), cot_send.at[c, step], cot_recv.at[c, t], {"tp": mate(step)})

    def partner_copy(c, step):
        b = mate(step)
        return remote(
            cot_block(c, b), cot_block(c, b), cot_send.at[c, pairs + step], cot_recv.at[c, b], {"tp": partner}
        )

    def share_cot(c):
        cot_copy(c).wait_recv()
        for step in range(1, pairs):
            mate_copy(c, step).start()
        partner_copy(c, 0).start()
        for step in range(1, pairs):
            partner_copy(c, step).wait_recv()
            partner_copy(c, step).start()
        for step in range(pairs):
            b = lax.rem(y + step, pairs) * 2 + (1 - core)
            remote(cot_block(c, b), cot_block(c, b), cot_send.at[c, 0], cot_recv.at[c, b], {"tp": partner}).wait_recv()

    def up_copy(k, c):
        return remote(term.at[k, c], recv.at[k, c + 1], send_sem.at[k, c], recv_sem.at[k, c + 1], {"fsdp": lax.rem(f + 1, n)})

    def down_copy(k, c):
        return remote(term.at[k, c], recv.at[k, c], send_sem.at[k, c], recv_sem.at[k, c], {"fsdp": lax.rem(f + n - 1, n)})

    def arrived(k, slot):
        remote(term.at[k, 0], recv.at[k, slot], send_sem.at[k, 0], recv_sem.at[k, slot], {"fsdp": lax.rem(f + 1, n)}).wait_recv()

    def compute(k, opening):
        own_copy(k).wait()
        if not opening:
            hidden_copy(k).wait_recv()

        def one(i, _):
            c = order(i)
            if opening:
                share_cot(c)

                @pl.when(i == 0)
                def _():
                    hidden_copy(k).wait_recv()

            cols = pl.ds(pl.multiple_of(c * rows, rows), rows)
            value = lax.dot_general(
                cot[pl.ds(0, tokens), cols], own[k], TOKENS_FIRST, preferred_element_type=jnp.float32
            ) + lax.dot_general(
                cot[pl.ds(tokens, tokens), cols], other[k], TOKENS_FIRST, preferred_element_type=jnp.float32
            )
            term[k, c] = value.astype(jnp.bfloat16)

            @pl.when((f == 0) & (c > 0))
            def _():
                up_copy(k, c).start()

            @pl.when((f == n - 1) & (c < n - 1))
            def _():
                down_copy(k, c).start()

            return 0

        lax.fori_loop(0, n, one, 0)

    def relay(k):
        def one(i, _):
            c = n - 1 - i

            @pl.when((f > 0) & (c > f))
            def _():
                arrived(k, c + 1)
                term[k, c] = term[k, c] + recv[k, c + 1]
                up_copy(k, c).start()

            @pl.when((f < n - 1) & (i < f))
            def _():
                arrived(k, i)
                term[k, i] = term[k, i] + recv[k, i]
                down_copy(k, i).start()

            return 0

        lax.fori_loop(0, n, one, 0)

    def out_copy(k):
        return pltpu.make_async_copy(
            total, new_hbm.at[:, pl.ds(pl.multiple_of(k * width, width), width)], out_sem.at[0]
        )

    def in_copies(k):
        cols = pl.ds(pl.multiple_of(k * width, width), width)
        return (
            pltpu.make_async_copy(momentum_hbm.at[:, cols], held, in_sem.at[0]),
            pltpu.make_async_copy(weight_hbm.at[:, cols], master, in_sem.at[1]),
        )

    def finish(k):
        @pl.when(f > 0)
        def _():
            arrived(k, f + 1)

        @pl.when(f < n - 1)
        def _():
            arrived(k, f)

        @pl.when(k > 0)
        def _():
            out_copy(k).wait()

        total[...] = term[k, f].astype(jnp.float32)

        @pl.when(f > 0)
        def _():
            total[...] += recv[k, f + 1].astype(jnp.float32)

        @pl.when(f < n - 1)
        def _():
            total[...] += recv[k, f].astype(jnp.float32)

        for copy in in_copies(k):
            copy.wait()
        total[...] += MOMENTUM * held[...]
        out_copy(k).start()
        weight = (master[...] - LEARN_RATE * total[...]).astype(jnp.bfloat16)
        acc[...] += lax.dot_general(
            rolls[:, pl.ds(pl.multiple_of(k * width, width), width)],
            weight, (((1,), (1,)), ((), ())), preferred_element_type=jnp.float32,
        )

    own_cot.wait()
    compute(0, True)
    own_roll.wait()
    for step in range(1, n):
        roll_arrived(g * n + lax.rem(f + step, n))
    for step in range(n):
        cross_copy(step).start()
    lax.fori_loop(early, chunks, start_hidden, 0)
    acc[...] = jnp.zeros_like(acc)

    lag = jnp.where((f == 0) | (f == n - 1), END_LAG, MID_LAG)

    def iteration(it, _):
        @pl.when((it >= lag) & (it < chunks + lag))
        def _():
            for copy in in_copies(it - lag):
                copy.start()

        @pl.when(it < chunks)
        def _():
            compute(it, False)

        @pl.when((it >= 1) & (it <= chunks))
        def _():
            relay(it - 1)

        @pl.when(it == lag)
        def _():
            for step in range(n):
                roll_arrived((1 - g) * n + lax.rem(f + step, n))

        @pl.when((it >= lag) & (it < chunks + lag))
        def _():
            finish(it - lag)

        return 0

    lax.fori_loop(1, chunks + END_LAG, iteration, 0)

    tails = []
    for d in range(groups):
        parts[d] = acc[d * batch:(d + 1) * batch, :].astype(jnp.bfloat16)
    for step in range(1, groups):
        d = lax.rem(me + step, groups)
        tails.append(remote(parts.at[d], landed.at[me], tail_send.at[len(tails)], all_recv.at[me], place(d)))
        tails[-1].start()
    landed[me] = parts[me]
    for step in range(1, groups):
        d = lax.rem(me + step, groups)
        remote(parts.at[d], landed.at[d], tail_send.at[0], all_recv.at[d], place(d)).wait_recv()
    per = groups // n_tp
    mine = pl.ds(t * per, per)
    for step in range(1, n_tp):
        b = lax.rem(t + step, n_tp)
        tails.append(
            remote(landed.at[pl.ds(b * per, per)], reduced.at[t], tail_send.at[len(tails)], sum_recv.at[t], {"tp": b})
        )
        tails[-1].start()
    value = landed[mine].astype(jnp.float32)
    for step in range(1, n_tp):
        b = lax.rem(t + step, n_tp)
        remote(landed.at[mine], reduced.at[b], tail_send.at[0], sum_recv.at[b], {"tp": b}).wait_recv()
        value = value + reduced[b].astype(jnp.float32)
    final[mine] = value.astype(jnp.bfloat16)
    for step in range(1, n_tp):
        b = lax.rem(t + step, n_tp)
        tails.append(remote(final.at[mine], final.at[mine], tail_send.at[len(tails)], gather_recv.at[t], {"tp": b}))
        tails[-1].start()
    for step in range(1, n_tp):
        b = lax.rem(t + step, n_tp)
        theirs = pl.ds(b * per, per)
        remote(final.at[theirs], final.at[theirs], tail_send.at[0], gather_recv.at[b], {"tp": b}).wait_recv()
    for d in range(groups):
        out_ref[:, d * rows:(d + 1) * rows] = final[d]

    out_copy(0).wait()
    for copy in tails:
        copy.wait_send()
    for step in range(1, n):
        roll_copy(step).wait_send()
    for step in range(n):
        cross_copy(step).wait_send()

    def drain_cot(c, _):
        cot_copy(c).wait_send()
        for step in range(1, pairs):
            mate_copy(c, step).wait_send()
        for step in range(pairs):
            partner_copy(c, step).wait_send()
        return 0

    lax.fori_loop(0, n, drain_cot, 0)

    def drain(k, _):
        hidden_copy(k).wait_send()

        def one(c, _):
            @pl.when(c != f)
            def _():
                up_copy(k, c).wait_send()

            return 0

        return lax.fori_loop(0, n, one, 0)

    lax.fori_loop(0, chunks, drain, 0)


def local(n_grp, n_fsdp, n_tp, learn_hidden, learn_cotangent, master_weight, momentum, roll_hidden):
    tokens, features = learn_cotangent.shape
    units = learn_hidden.shape[1]
    rows = features // n_grp // n_fsdp
    width = 256
    chunks = units // width
    pairs = n_tp // 2
    groups = n_grp * n_fsdp
    batch = roll_hidden.shape[0]
    dma = pltpu.SemaphoreType.DMA
    small, wide = jnp.bfloat16, jnp.float32
    return tuple(pl.pallas_call(
        functools.partial(step_kernel, n_fsdp, n_tp),
        out_shape=(
            jax.ShapeDtypeStruct((rows, units), wide),
            jax.ShapeDtypeStruct((batch, features), small),
        ),
        in_specs=[pl.BlockSpec(memory_space=pl.ANY)] * 5,
        out_specs=(pl.BlockSpec(memory_space=pl.ANY), pl.BlockSpec(memory_space=pltpu.VMEM)),
        scratch_shapes=[
            pltpu.VMEM((n_grp * tokens, features // n_grp), small),
            pltpu.VMEM((chunks, tokens, width), small),
            pltpu.VMEM((chunks, tokens, width), small),
            pltpu.VMEM((chunks, n_fsdp, rows, width), small),
            pltpu.VMEM((chunks, n_fsdp + 1, rows, width), small),
            pltpu.VMEM((rows, width), wide),
            pltpu.VMEM((rows, width), wide),
            pltpu.VMEM((rows, width), wide),
            pltpu.VMEM((groups * batch, units), small),
            pltpu.VMEM((groups * batch, rows), wide),
            pltpu.VMEM((groups, batch, rows), small),
            pltpu.VMEM((groups, batch, rows), small),
            pltpu.VMEM((n_tp, groups // n_tp, batch, rows), small),
            pltpu.VMEM((groups, batch, rows), small),
            dma((1,)),
            dma((chunks,)),
            dma((n_fsdp, 2 * pairs)),
            dma((n_fsdp, n_tp)),
            dma((chunks,)),
            dma((chunks,)),
            dma((chunks, n_fsdp)),
            dma((chunks, n_fsdp + 1)),
            dma((1,)),
            dma((3,)),
            dma((2 * n_fsdp,)),
            dma((groups,)),
            dma((groups + 2 * n_tp,)),
            dma((groups,)),
            dma((n_tp,)),
            dma((n_tp,)),
        ],
        compiler_params=pltpu.CompilerParams(
            collective_id=0, has_side_effects=True, vmem_limit_bytes=60 * 1024 * 1024
        ),
        name="learner_step",
    )(learn_cotangent, learn_hidden, master_weight, momentum, roll_hidden))


def solution(mesh):
    blocks = P(("grp", "fsdp"), "tp")
    whole_rows = P(("grp", "fsdp"), None)
    sizes = (mesh.shape["grp"], mesh.shape["fsdp"], mesh.shape["tp"])
    return jax.shard_map(
        functools.partial(local, *sizes),
        mesh=mesh,
        in_specs=(blocks, whole_rows, blocks, blocks, blocks),
        out_specs=(blocks, whole_rows),
        check_vma=False,
    )
```

time: 388 us -> 322 us (0.83)
  waiting for transfers between devices: 30 us -> 0 us
  between operations: 14.1 us -> 0.65 us
  blocking collectives: 11.2 us -> 0 us
  other arithmetic: 9.68 us -> 0 us
  matrix products: 6.86 us -> 0 us
  local copies, waits for them, and re-layouts: 2.39 us -> 7.35 us
    psum x1 -> x0, waiting for transfers between devices: 29.3 us -> none  [local(): roll_out = lax.psum(spread, 'tp')]
    all_to_all x1 -> x0, blocking collectives: 11.2 us -> none  [local(): lax.all_to_all(partial_out, ('grp', 'fsdp'), split_axis=0, concat_axis=1,...]
    add x1 -> x0, other arithmetic: 9.68 us -> none  [local(): momentum_new = MOMENTUM * momentum + grad]
    dot_general x1 -> x0, matrix products: 6.86 us -> none  [local(): lax.dot_general(roll_all, rollout_weight, (((1,), (1,)), ((), ())), prefe...]
    unnamed x1 -> x4, local copies, waits for them, and re-layouts: 1.67 us -> 7.35 us
  transfers between devices with their start and end apart: 2 -> 0, of which waited for: 1 -> 0; matrix products, arithmetic and copies ran while one was open for 2% -> 0% of each run, Pallas kernels for 81% -> 0%
where the time goes in v2:
time: 322 us; the launch traced here: 321 us
  Pallas kernels  313 us (97%)
  local copies, waits for them, and re-layouts  7.35 us (2%)
    pallas_call x1, Pallas kernels, local(): pl.pallas_call(functools.partial(step_kernel, n_fsdp, n_tp), out_shape=(j...  313 us
    unnamed x4, local copies, waits for them, and re-layouts  7.35 us

profile of v2, /device:TPU:0, one launch (start us, length us, event | category | flops | bytes accessed | tf_op | source)
XLA Modules:
  0.0 321.3 jit_solution(8880203398958369269)
XLA Ops:
  0.6 313.3 %learner_step.1 = (f32[512,3584]{1,0:T(8,128)}, bf16[32,4096]{1,0:T(8,128)(2,1)}) custom-call(bf16[1024,4096]{1,0:T(8,128)(2,1)} %cot_hbm.1, bf16[1024,3584]{1,0:T(8,128)(2,1)} %hid_hbm.1, f32[512,3584]{1,0:T(8,128)} %weight_hbm.1, f32[512,3584]{1,0:T(8,128)} %momentum_hbm.1, bf16[32,3584]{1,0:T(8,128)(2,1)} %roll_hbm.1), custom_call_target="tpu_custom_call" | custom-call | tf_op jit(solution)/shard_map/learner_step/pallas_call | solution.py:373
  314.0 0.0 copy-start
  314.0 6.6 %copy.9 = f32[512,3584]{1,0:T(8,128)} copy(f32[512,3584]{1,0:T(8,128)} %get-tuple-element.4) | data formatting | bytes 14680064
  320.6 0.0 copy-done
  320.6 0.7 copy.10
Async XLA Ops:
  314.0 6.7 %copy-start = (bf16[32,4096]{1,0:T(8,128)(2,1)S(1)}, bf16[32,4096]{1,0:T(8,128)(2,1)}, u32[]{:S(2)}) copy-start(bf16[32,4096]{1,0:T(8,128)(2,1)} %get-tuple-element.5) | copy-start | bytes 786436
